TPU v7x, 32 devices: a whole 2x2x4 slice. The times are simulated.
32 devices in a mesh: head: 2 (over y), seq: 16 (over z, x, core).
Axes of the slice: x: 2, y: 2, z: 4, core: 2. Of those that a mesh axis runs over, the one named last changes fastest.
Arguments:
- keys: bfloat16 [65536, 128], P(('head', 'seq')), parts along dimension 0, may hold values from -6 to 6
- values: bfloat16 [65536, 128], P(('head', 'seq')), parts along dimension 0, may hold values from -6 to 6
- queries: bfloat16 [65536, 128], P(('head', 'seq')), parts along dimension 0, may hold values from -160 to 160
- query_positions: int32 [256], P(('head', 'seq')), parts along dimension 0, may hold values from 0 to 32767, as said below
- kept_index: int32 [1024], P('head'), parts along dimension 0, may hold values from 0 to 32767, as said below
- ridge_level: int32 [2], P('head'), parts along dimension 0, may hold values from 20 to 99
Outputs:
- matched_values: float32 [1024, 128], P('head'), parts along dimension 0
- ref_out: float32 [256, 128], P(('head', 'seq')), parts along dimension 0
There are 2 independent parts, one for each index of `head`. A program takes and returns all parts, laid end to end along the dimension named above; each array names one. Nothing has to cross between parts.
Inputs may be any that keep to these rules, and one draw needn't show every extreme that they name: `query_positions`: entries 8 d to 8 (d + 1) - 1 are distinct increasing positions within the slab of positions 2048 d to 2048 (d + 1) - 1. `kept_index`: distinct and increasing.
All inputs are finite; a program needn't handle non-finite values.
Results may differ from a plain program's by a relative error of at most 0.00051.
Values may be sent and summed in bfloat16 or wider, within the bound.
A program may use at most 64 MiB of HBM per device.

v0:
```python
import math

import jax
import jax.numpy as jnp
from jax import lax
from jax.sharding import PartitionSpec as P


def combined_all(x, axis, combine):
    everything = jax.tree.map(lambda part: lax.all_gather(part, axis), x)
    first = jax.tree.map(lambda part: part[0], everything)

    def turn(k, so_far):
        return combine(so_far, jax.tree.map(lambda part: part[k], everything))

    return lax.fori_loop(1, lax.axis_size(axis), turn, first)


def combine_partials(earlier, later):
    peak_a, total_a, numer_a = earlier
    peak_b, total_b, numer_b = later
    joined = jnp.maximum(peak_a, peak_b)
    factor_a = jnp.exp(peak_a - joined)
    factor_b = jnp.exp(peak_b - joined)
    return (
        joined,
        total_a * factor_a + total_b * factor_b,
        numer_a * factor_a[:, None] + numer_b * factor_b[:, None],
    )


def per_device(keys, values, queries, query_positions, kept_index, ridge_level):
    slab_len = keys.shape[0]
    head_dim = keys.shape[1]
    own_count = query_positions.shape[0]
    inv_root = 1.0 / math.sqrt(head_dim)
    slab_start = lax.axis_index("seq") * slab_len
    local_rows = query_positions - slab_start
    own_queries = jnp.take(queries, local_rows, axis=0)
    all_queries = lax.all_gather(own_queries, "seq", axis=0, tiled=True)
    offset = kept_index - slab_start
    inside = ((offset >= 0) & (offset < slab_len)).astype(jnp.float32)
    picked = (
        jnp.take(keys, jnp.clip(offset, 0, slab_len - 1), axis=0).astype(jnp.float32)
        * inside[:, None]
    )
    kept_keys = lax.psum(picked, "seq").astype(jnp.bfloat16)
    full_logits = jnp.dot(all_queries, kept_keys.T, preferred_element_type=jnp.float32) * inv_root
    weights = jax.nn.softmax(full_logits, axis=1)
    gram_local = jnp.dot(weights.T, weights, precision=lax.Precision.HIGHEST)
    row_count = all_queries.shape[0]
    row_block = math.gcd(row_count, 512)

    def block_partials(query_block):
        scores = jnp.dot(query_block, keys.T, preferred_element_type=jnp.float32) * inv_root
        row_peak = jnp.max(scores, axis=1)
        probs = jnp.exp(scores - row_peak[:, None]).astype(jnp.bfloat16)
        totals = jnp.sum(probs.astype(jnp.float32), axis=1)
        numer = jnp.dot(probs, values, preferred_element_type=jnp.float32)
        return (row_peak, totals, numer)

    peaks, totals, numers = lax.map(
        block_partials, all_queries.reshape(row_count // row_block, row_block, head_dim)
    )
    peaks = peaks.reshape(row_count)
    totals = totals.reshape(row_count)
    numers = numers.reshape(row_count, head_dim)
    own_start = lax.axis_index("seq") * own_count
    merged_peak, merged_total, merged_numer = combined_all(
        (peaks, totals, numers), "seq", combine_partials
    )
    full_ref = merged_numer / merged_total[:, None]
    ref_out = lax.dynamic_slice_in_dim(full_ref, own_start, own_count, 0)
    moment = jnp.dot(weights.T, full_ref, precision=lax.Precision.HIGHEST)
    ridge_value = ridge_level[0].astype(jnp.float32) * 0.01
    system = gram_local + ridge_value * jnp.eye(gram_local.shape[0], dtype=jnp.float32)
    lower = jnp.linalg.cholesky(system)
    matched_values = jax.scipy.linalg.cho_solve((lower, True), moment)
    return (matched_values, ref_out)


def solution(mesh):
    placed = (
        P(("head", "seq"), None),
        P(("head", "seq"), None),
        P(("head", "seq"), None),
        P(("head", "seq")),
        P("head"),
        P("head"),
    )
    return jax.shard_map(
        per_device,
        mesh=mesh,
        in_specs=placed,
        out_specs=(P("head", None), P(("head", "seq"), None)),
        check_vma=False,
    )
```

profile of v0, /device:TPU:0, one launch (start us, length us, event | category | flops | bytes accessed | tf_op | source)
XLA Modules:
  0.0 308.4 jit_solution(11675283586581244376)
XLA Ops:
  7.9 1.7 gather_fusion
  9.7 23.2 %all_gather.12 = bf16[128,128]{1,0:T(8,128)(2,1)S(1)} all-gather(bf16[8,128]{1,0:T(8,128)(2,1)S(1)} %broadcast_select_fusion), channel_id=1, replica_groups=mesh['head'=2,'seq'=16] {'seq'}, dimensions={0}, use_global_device_ids=true | all-gather | bytes 34816 | tf_op jit(solution)/shard_map/all_gather | solution.py:40
  33.9 1.0 fusion.61
  35.6 1.3 gather_fusion.1
  37.2 60.6 %all-reduce.2 = bf16[512,128]{1,0:T(8,128)(2,1)S(1)} all-reduce(f32[512,128]{1,0:T(8,128)S(1)} %convert_multiply_fusion), channel_id=1, replica_groups=mesh['head'=2,'seq'=16] {'seq'}, use_global_device_ids=true, to_apply=%region_0.1 | all-reduce | flops 65536 | bytes 393216 | tf_op jit(solution)/shard_map/psum | solution.py:47
  98.2 1.1 fusion.59
  99.4 1.4 copy.9
  101.4 1.4 fusion.7
  102.9 1.0 copy-done.2
  103.9 11.7 %cholesky.103 = f32[128,128]{1,0:T(8,128)S(1)} custom-call(f32[128,128]{1,0:T(8,128)S(1)} %cholesky.263), custom_call_target="Cholesky" | custom-call | tf_op jit(solution)/shard_map/jit(cholesky)/cholesky | solution.py:77
  115.8 9.8 %custom-call.34 = f32[1,128,128]{1,2,0:T(8,128)S(1)} custom-call(f32[1,128,128]{2,1,0:T(8,128)S(1)} %get-tuple-element.251), custom_call_target="InvertDiagBlocksLowerTriangular" | custom-call | tf_op jit(solution)/shard_map/jit(cholesky)/cholesky | solution.py:77
  125.6 1.2 constant_dynamic-update-slice_fusion.3
  126.9 1.3 convolution_subtract_fusion
  128.1 11.7 %cholesky.215 = f32[128,128]{1,0:T(8,128)S(1)} custom-call(f32[128,128]{1,0:T(8,128)S(1)} %cholesky.267), custom_call_target="Cholesky" | custom-call | tf_op jit(solution)/shard_map/jit(cholesky)/cholesky | solution.py:77
  140.1 9.8 %custom-call.35 = f32[1,128,128]{1,2,0:T(8,128)S(1)} custom-call(f32[1,128,128]{2,1,0:T(8,128)S(1)} %get-tuple-element.248), custom_call_target="InvertDiagBlocksLowerTriangular" | custom-call | tf_op jit(solution)/shard_map/jit(cholesky)/cholesky | solution.py:77
  150.2 1.3 convolution_subtract_fusion.1
  151.5 11.7 %cholesky.236 = f32[128,128]{1,0:T(8,128)S(1)} custom-call(f32[128,128]{1,0:T(8,128)S(1)} %cholesky.272), custom_call_target="Cholesky" | custom-call | tf_op jit(solution)/shard_map/jit(cholesky)/cholesky | solution.py:77
  163.2 9.8 %custom-call.36 = f32[1,128,128]{1,2,0:T(8,128)S(1)} custom-call(f32[1,128,128]{2,1,0:T(8,128)S(1)} %get-tuple-element.245), custom_call_target="InvertDiagBlocksLowerTriangular" | custom-call | tf_op jit(solution)/shard_map/jit(cholesky)/cholesky | solution.py:77
  173.2 1.2 convolution_subtract_fusion.8
  174.5 11.9 %cholesky.253 = f32[128,128]{1,0:T(8,128)S(1)} custom-call(f32[128,128]{1,0:T(8,128)S(1)} %convolution_subtract_fusion.8), custom_call_target="Cholesky" | custom-call | tf_op jit(solution)/shard_map/jit(cholesky)/cholesky | solution.py:77
  191.0 1.2 select_select_fusion
  192.1 11.4 %while.27 = (s32[]{:T(128)}, f32[512,512]{1,0:T(8,128)}, s32[4,2]{0,1:T(2,128)S(1)}, f32[4,128,128]{2,1,0:T(8,128)S(1)}, s32[]{:T(128)}) while((s32[]{:T(128)}, f32[512,512]{1,0:T(8,128)}, s32[4,2]{0,1:T(2,128)S(1)}, f32[4,128,128]{2,1,0:T(8,128)S(1)}, s32[]{:T(128)}) %tuple.77), condition=%wide.while_cond, body=%wide.while_body.sunk | while | flops 2 | bytes 131189 | solution.py:78
  192.8 2.2 bitcast_dynamic-update-slice_fusion.2
  195.6 2.2 bitcast_dynamic-update-slice_fusion.2
  198.5 2.2 bitcast_dynamic-update-slice_fusion.2
  201.4 2.2 bitcast_dynamic-update-slice_fusion.2
  203.5 39.3 %custom-call.37 = f32[4,128,128]{1,2,0:T(8,128)S(1)} custom-call(f32[4,128,128]{2,1,0:T(8,128)S(1)} %get-tuple-element.209), custom_call_target="InvertDiagBlocksLowerTriangular" | custom-call | tf_op jit(solution)/shard_map/jit(_cho_solve)/triangular_solve | solution.py:78
  242.9 17.1 %all-gather.3 = f32[16,1,128]{2,1,0:T(1,128)S(1)} all-gather(f32[1,1,128]{2,1,0:T(1,128)S(1)} %bitcast.100), channel_id=2, replica_groups=mesh['head'=2,'seq'=16] {'seq'}, dimensions={0}, use_global_device_ids=true | all-gather | bytes 8704 | tf_op jit(solution)/shard_map/all_gather | solution.py:10
  260.3 19.1 %all-gather.4 = f32[16,1,128]{2,1,0:T(1,128)S(1)} all-gather(f32[1,1,128]{2,1,0:T(1,128)S(1)} %bitcast.101), channel_id=3, replica_groups=mesh['head'=2,'seq'=16] {'seq'}, dimensions={0}, use_global_device_ids=true | all-gather | bytes 8704 | tf_op jit(solution)/shard_map/all_gather | solution.py:10
  280.3 15.2 %while.26 = (s32[]{:T(128)}, f32[128]{0:T(128)S(1)}, f32[128]{0:T(128)S(1)}, f32[128,128]{1,0:T(8,128)S(1)}, f32[16,128]{1,0:T(8,128)S(1)}, /*index=5*/f32[16,12...) while((s32[]{:T(128)}, f32[128]{0:T(128)S(1)}, f32[128]{0:T(128)S(1)}, ...), condition=%wide.region_14.15_spmd, body=%wide.region_13.14_spmd.sunk | while | flops 49925 | bytes 201879 | solution.py:16
  280.3 1.0 fusion.86
  281.4 1.0 fusion.86
  (97 shorter events, 28.7 us)
Async XLA Ops:
  7.2 25.7 %copy-start = (bf16[2048,128]{1,0:T(8,128)(2,1)S(1)}, bf16[2048,128]{1,0:T(8,128)(2,1)}, u32[]{:S(2)}) copy-start(bf16[2048,128]{1,0:T(8,128)(2,1)} %param.8) | copy-start | bytes 1572868
  7.2 272.2 %all-gather.7.cloned.1.call-start = ((), (), s32[]{:S(2)}) async-start(), calls=%async_computation | async-start | bytes 1114112 | tf_op jit(solution)/shard_map/all_gather | solution.py:10
  7.2 0.7 copy-start.5
  32.9 1.0 copy-start.3
  34.9 0.7 copy-start.4
  102.9 1.0 copy-start.2
  280.2 16.3 %copy-start.1 = (f32[512,512]{1,0:T(8,128)S(1)}, f32[512,512]{1,0:T(8,128)}, u32[]{:S(2)}) copy-start(f32[512,512]{1,0:T(8,128)} %get-tuple-element.387) | copy-start | bytes 3145732
Sparse Core Ops, SparseCore 0:
  35.0 35.7 all-gather.6
where the time goes:
time: 310 us; the launch traced here: 308 us
  other arithmetic  137 us (44%)
  blocking collectives  120 us (39%)
  local copies, waits for them, and re-layouts  20.4 us (7%)
  between operations  17.5 us (6%)
  matrix products  12.8 us (4%)
    another operation x14, other arithmetic, per_device(): lower = jnp.linalg.cholesky(system)  78.8 us
    psum x1, blocking collectives, per_device(): kept_keys = lax.psum(picked, 'seq').astype(jnp.bfloat16)  60.6 us
    another operation x4, other arithmetic, per_device(): matched_values = jax.scipy.linalg.cho_solve((lower, True), moment)  41.2 us
    all_gather x2, blocking collectives, combined_all(): everything = jax.tree.map(lambda part: lax.all_gather(part, axis), x)  36.2 us
    all_gather x1, blocking collectives, per_device(): all_queries = lax.all_gather(own_queries, 'seq', axis=0, tiled=True)  23.2 us
    add x15, other arithmetic, combine_partials(): numer_a * factor_a[:, None] + numer_b * factor_b[:, None]  14.4 us
    another operation x12, local copies, waits for them, and re-layouts  11.3 us
  transfers between devices with their start and end apart: 1, of which 0 were waited for; matrix products, arithmetic and copies ran while one was open for 46% of the time, Pallas kernels for 0%

commit v1 on v0

v1 whole, which is shorter than its diff:
```python
import functools
import math

import jax
import jax.numpy as jnp
from jax import lax
from jax.experimental import pallas as pl
from jax.experimental.pallas import tpu as pltpu
from jax.sharding import PartitionSpec as P

MESH = pl.DeviceIdType.MESH
HIGH = lax.Precision.HIGHEST
LANES = 128
SUB = 8


def nt(a, b, precision=None):
    return lax.dot_general(
        a, b, (((1,), (1,)), ((), ())), precision=precision, preferred_element_type=jnp.float32
    )


def inverse_block(m):
    sub = lax.broadcasted_iota(jnp.int32, (SUB, LANES), 0)
    lane = lax.broadcasted_iota(jnp.int32, (SUB, LANES), 1)
    wide_lane = lax.broadcasted_iota(jnp.int32, (LANES, LANES), 1)
    for s in range(0, LANES, SUB):
        rows = m[s : s + SUB, :]
        cols = [jnp.broadcast_to(rows[:, s + j : s + j + 1], (SUB, LANES)) for j in range(SUB)]
        inside = (lane >= s) & (lane < s + SUB)
        work = jnp.where(inside, jnp.where(lane - s == sub, 1.0, 0.0), rows)
        for i in range(SUB):
            here = sub == i
            factor = cols[i]
            pivot = 1.0 / factor[i : i + 1, :]
            for j in range(i + 1, SUB):
                scaled = cols[j][i : i + 1, :] * pivot
                cols[j] = jnp.where(here, scaled, cols[j] - factor * scaled)
            scaled = work[i : i + 1, :] * pivot
            work = jnp.where(here, scaled, work - factor * scaled)
        panel = m[:, s : s + SUB]
        cleared = jnp.where((wide_lane >= s) & (wide_lane < s + SUB), 0.0, m)
        m = cleared - jnp.dot(panel, work, precision=HIGH, preferred_element_type=jnp.float32)
        parts = ([m[:s]] if s else []) + [work] + ([m[s + SUB :]] if s + SUB < LANES else [])
        m = jnp.concatenate(parts, axis=0)
    return m


def invert(s_ref):
    count = s_ref.shape[0]
    if count == LANES:
        s_ref[...] = inverse_block(s_ref[...])
        return

    def turn(k, carry):
        at = pl.ds(pl.multiple_of(k * LANES, LANES), LANES)
        inner = inverse_block(s_ref[at, at])
        s_ref[at, :] = jnp.dot(inner, s_ref[at, :], precision=HIGH, preferred_element_type=jnp.float32)
        s_ref[at, at] = inner

        def row(r, c):
            other = pl.ds(pl.multiple_of(r * LANES, LANES), LANES)

            @pl.when(r != k)
            def _():
                panel = s_ref[other, at]
                s_ref[other, at] = jnp.zeros((LANES, LANES), jnp.float32)
                s_ref[other, :] = s_ref[other, :] - jnp.dot(
                    panel, s_ref[at, :], precision=HIGH, preferred_element_type=jnp.float32
                )

            return c

        return lax.fori_loop(0, count // LANES, row, carry)

    lax.fori_loop(0, count // LANES, turn, 0)


def kernel(
    n,
    pos_ref,
    level_ref,
    kept_ref,
    keys_hbm,
    values_hbm,
    queries_hbm,
    matched_ref,
    ref_ref,
    keys,
    values,
    queries,
    own_q,
    all_q,
    pick,
    pick_in,
    chunk,
    kept_all,
    part,
    part_in,
    own_ref,
    all_ref,
    system,
    load_sem,
    send_sem,
    recv_sem,
):
    me = lax.axis_index("seq")
    slab, head_dim = keys.shape
    own = own_q.shape[0]
    count = n * own
    keep = kept_ref.shape[0] * kept_ref.shape[1]
    each = keep // n
    inv_root = 1.0 / math.sqrt(head_dim)
    start = me * slab

    loads = [
        pltpu.make_async_copy(src, dst, load_sem.at[k])
        for k, (src, dst) in enumerate(((queries_hbm, queries), (keys_hbm, keys), (values_hbm, values)))
    ]
    for load in loads:
        load.start()

    def peer(k):
        return lax.rem(me + k, n)

    barrier = pltpu.get_barrier_semaphore()

    def greet(k, c):
        pl.semaphore_signal(barrier, inc=1, device_id={"seq": peer(k)}, device_id_type=MESH)
        return c

    lax.fori_loop(1, n, greet, 0)

    def copy_of(stage, k, src, dst):
        return pltpu.make_async_remote_copy(
            src_ref=src(peer(k)),
            dst_ref=dst.at[me],
            send_sem=send_sem.at[stage, k],
            recv_sem=recv_sem.at[stage, k],
            device_id={"seq": peer(k)},
            device_id_type=MESH,
        )

    def send(stage, src, dst):
        def one(k, c):
            copy_of(stage, k, src, dst).start()
            return c

        lax.fori_loop(1, n, one, 0)

    def arrive(stage, src, dst):
        def one(k, c):
            copy_of(stage, k, src, dst).wait_recv()
            return c

        lax.fori_loop(1, n, one, 0)

    def sent(stage, src, dst):
        def one(k, c):
            copy_of(stage, k, src, dst).wait_send()
            return c

        lax.fori_loop(1, n, one, 0)

    q_args = (0, lambda p: own_q, all_q)
    pick_args = (1, lambda p: pick.at[p], pick_in)
    kept_args = (2, lambda p: chunk, kept_all)
    part_args = (3, lambda p: part.at[p], part_in)
    ref_args = (4, lambda p: own_ref, all_ref)

    loads[0].wait()
    sub = lax.broadcasted_iota(jnp.int32, (own, slab), 0)
    wanted = jnp.zeros((own, slab), jnp.int32)
    for i in range(own):
        wanted = jnp.where(sub == i, pos_ref[i] - start, wanted)
    chosen = wanted == lax.broadcasted_iota(jnp.int32, (own, slab), 1)
    rows = jnp.dot(
        jnp.where(chosen, 1.0, 0.0).astype(jnp.bfloat16), queries[...], preferred_element_type=jnp.float32
    )
    own_q[...] = rows
    all_q[me] = rows

    loads[1].wait()
    places = lax.broadcasted_iota(jnp.int32, (LANES, slab), 1).astype(jnp.float32)
    for j in range(keep // LANES):
        offset = (kept_ref[j : j + 1, :] - start).astype(jnp.float32)
        offset = jnp.broadcast_to(offset, (LANES, LANES)).T
        chosen = jnp.where(jnp.concatenate([offset] * (slab // LANES), axis=1) == places, 1.0, 0.0)
        found = jnp.dot(chosen.astype(jnp.bfloat16), keys[...], preferred_element_type=jnp.float32)
        pick[pl.ds(j * LANES // each, LANES // each)] = found.astype(pick.dtype).reshape(
            LANES // each, each, head_dim
        )
    pick_in[me] = pick[me]

    pl.semaphore_wait(barrier, n - 1)
    send(*q_args)
    send(*pick_args)
    arrive(*q_args)
    all_queries = all_q[...].reshape(count, head_dim).astype(jnp.bfloat16)
    arrive(*pick_args)
    total = pick_in[0].astype(jnp.float32)
    for k in range(1, n):
        total = total + pick_in[k].astype(jnp.float32)
    chunk[...] = total.astype(chunk.dtype)
    kept_all[me] = total.astype(chunk.dtype)
    send(*kept_args)

    loads[2].wait()
    scores = nt(all_queries, keys[...]) * inv_root
    peak = jnp.max(scores, axis=1, keepdims=True)
    probs = jnp.exp(scores - peak).astype(jnp.bfloat16)
    totals = jnp.sum(probs.astype(jnp.float32), axis=1, keepdims=True)
    numer = jnp.dot(probs, values[...], preferred_element_type=jnp.float32)
    half = lax.broadcasted_iota(jnp.int32, (count, LANES), 1) < LANES // 2
    part[:, :, :head_dim] = numer.reshape(n, own, head_dim)
    part[:, :, head_dim:] = jnp.where(half, peak, totals).reshape(n, own, LANES)
    part_in[me] = part[me]
    send(*part_args)

    arrive(*kept_args)
    kept_keys = kept_all[...].reshape(keep, head_dim).astype(jnp.bfloat16)
    logits = nt(all_queries, kept_keys) * inv_root
    weights = jnp.exp(logits - jnp.max(logits, axis=1, keepdims=True))
    weights = weights / jnp.sum(weights, axis=1, keepdims=True)

    arrive(*part_args)
    stats = part_in[:, :, head_dim:]
    peaks = stats[:, :, 0:1]
    sums = stats[:, :, LANES // 2 : LANES // 2 + 1]
    factors = jnp.exp(peaks - jnp.max(peaks, axis=0, keepdims=True))
    merged = jnp.sum(part_in[:, :, :head_dim] * factors, axis=0) / jnp.sum(sums * factors, axis=0)
    own_ref[...] = merged
    all_ref[me] = merged
    ref_ref[...] = merged
    send(*ref_args)

    ridge = level_ref[0].astype(jnp.float32) * 0.01
    eye = lax.broadcasted_iota(jnp.int32, (count, count), 0) == lax.broadcasted_iota(
        jnp.int32, (count, count), 1
    )
    system[...] = nt(weights, weights, HIGH) + jnp.where(eye, ridge, 0.0)
    invert(system)

    arrive(*ref_args)
    full_ref = all_ref[...].reshape(count, head_dim)
    inner = jnp.dot(system[...], full_ref, precision=HIGH, preferred_element_type=jnp.float32)
    matched_ref[...] = lax.dot_general(
        weights, inner, (((0,), (0,)), ((), ())), precision=HIGH, preferred_element_type=jnp.float32
    )
    for args in (q_args, pick_args, kept_args, part_args, ref_args):
        sent(*args)


def per_device(n, keys, values, queries, query_positions, kept_index, ridge_level):
    slab, head_dim = keys.shape
    own = query_positions.shape[0]
    keep = kept_index.shape[0]
    count = n * own
    each = keep // n
    link = jnp.bfloat16 if each % 16 == 0 else jnp.float32
    vmem = pl.BlockSpec(memory_space=pltpu.VMEM)
    smem = pl.BlockSpec(memory_space=pltpu.SMEM)
    hbm = pl.BlockSpec(memory_space=pl.ANY)
    f32 = jnp.float32
    return pl.pallas_call(
        functools.partial(kernel, n),
        out_shape=(
            jax.ShapeDtypeStruct((keep, head_dim), f32),
            jax.ShapeDtypeStruct((own, head_dim), f32),
        ),
        in_specs=[smem, smem, vmem, hbm, hbm, hbm],
        out_specs=(vmem, vmem),
        scratch_shapes=[
            pltpu.VMEM((slab, head_dim), keys.dtype),
            pltpu.VMEM((slab, head_dim), values.dtype),
            pltpu.VMEM((slab, head_dim), queries.dtype),
            pltpu.VMEM((own, head_dim), f32),
            pltpu.VMEM((n, own, head_dim), f32),
            pltpu.VMEM((n, each, head_dim), link),
            pltpu.VMEM((n, each, head_dim), link),
            pltpu.VMEM((each, head_dim), link),
            pltpu.VMEM((n, each, head_dim), link),
            pltpu.VMEM((n, own, head_dim + LANES), f32),
            pltpu.VMEM((n, own, head_dim + LANES), f32),
            pltpu.VMEM((own, head_dim), f32),
            pltpu.VMEM((n, own, head_dim), f32),
            pltpu.VMEM((count, count), f32),
            pltpu.SemaphoreType.DMA((3,)),
            pltpu.SemaphoreType.DMA((5, n)),
            pltpu.SemaphoreType.DMA((5, n)),
        ],
        compiler_params=pltpu.CompilerParams(
            collective_id=0, has_side_effects=True, vmem_limit_bytes=48 * 1024 * 1024
        ),
    )(
        query_positions,
        ridge_level,
        kept_index.reshape(keep // LANES, LANES),
        keys,
        values,
        queries,
    )


def solution(mesh):
    placed = (
        P(("head", "seq"), None),
        P(("head", "seq"), None),
        P(("head", "seq"), None),
        P(("head", "seq")),
        P("head"),
        P("head"),
    )
    return jax.shard_map(
        functools.partial(per_device, mesh.shape["seq"]),
        mesh=mesh,
        in_specs=placed,
        out_specs=(P("head", None), P(("head", "seq"), None)),
        check_vma=False,
    )
```

time: 310 us -> 35.6 us (0.11)
  other arithmetic: 137 us -> 0 us
  blocking collectives: 120 us -> 0 us
  Pallas kernels: 0 us -> 28.9 us
  between operations: 17.5 us -> 1.32 us
  local copies, waits for them, and re-layouts: 20.4 us -> 5.07 us
  matrix products: 12.8 us -> 0 us
    another operation x18 -> x0, other arithmetic: 120 us -> none  [the longest x14 78.8 us: per_device(): lower = jnp.linalg.cholesky(system)]
    psum x1 -> x0, blocking collectives: 60.6 us -> none  [per_device(): kept_keys = lax.psum(picked, 'seq').astype(jnp.bfloat16)]
    all_gather x3 -> x0, blocking collectives: 59.4 us -> none  [the longest x2 36.2 us: combined_all(): everything = jax.tree.map(lambda part: lax.all_gather(part, axis), x)]
    pallas_call x0 -> x1, Pallas kernels: none -> 28.9 us  [per_device(): pl.pallas_call(functools.partial(kernel, n), out_shape=(jax.ShapeDtypeStr...]
    add x30 -> x0, other arithmetic: 14.8 us -> none  [the longest x15 14.4 us: combine_partials(): numer_a * factor_a[:, None] + numer_b * factor_b[:, None]]
    another operation x17 -> x0, local copies, waits for them, and re-layouts: 11.5 us -> none
    another operation x20 -> x0, matrix products: 9.36 us -> none  [the longest x6 5.46 us: per_device(): lower = jnp.linalg.cholesky(system)]
    dot_general x5 -> x0, matrix products: 3.47 us -> none  [the longest x1 1.15 us: per_device(): gram_local = jnp.dot(weights.T, weights, precision=lax.Precision.HIGHEST)]
  transfers between devices with their start and end apart: 1 -> 0, of which waited for: 0 -> 0; matrix products, arithmetic and copies ran while one was open for 46% -> 0% of each run, Pallas kernels for 0% -> 0%
where the time goes in v1:
time: 35.6 us; the launch traced here: 35.3 us
  Pallas kernels  28.9 us (81%)
  local copies, waits for them, and re-layouts  5.07 us (14%)
  between operations  1.32 us (4%)
    pallas_call x1, Pallas kernels, per_device(): pl.pallas_call(functools.partial(kernel, n), out_shape=(jax.ShapeDtypeStr...  28.9 us
    unnamed x12, local copies, waits for them, and re-layouts  5.07 us

profile of v1, /device:TPU:0, one launch (start us, length us, event | category | flops | bytes accessed | tf_op | source)
XLA Modules:
  0.0 35.3 jit_solution(17323318853129188626)
XLA Ops:
  0.6 0.0 copy-start.3
  1.3 0.0 copy-start.4
  1.3 0.0 copy-done.3
  1.3 0.6 %copy-done.4 = s32[8]{0:T(128)S(1)} copy-done((s32[8]{0:T(128)S(1)}, s32[8]{0:T(128)}, u32[]{:S(2)}) %copy-start.4) | copy-done | bytes 56
  2.0 0.0 copy-start
  2.0 1.0 %copy-done = bf16[2048,128]{1,0:T(8,128)(2,1)S(1)} copy-done((bf16[2048,128]{1,0:T(8,128)(2,1)S(1)}, bf16[2048,128]{1,0:T(8,128)(2,1)}, u32[]{:S(2)}) %copy-start) | copy-done | bytes 524312
  3.0 0.0 copy-start.1
  3.0 1.0 %copy-done.1 = bf16[2048,128]{1,0:T(8,128)(2,1)S(1)} copy-done((bf16[2048,128]{1,0:T(8,128)(2,1)S(1)}, bf16[2048,128]{1,0:T(8,128)(2,1)}, u32[]{:S(2)}) %copy-start.1) | copy-done | bytes 524312
  4.0 0.0 copy-start.2
  4.0 1.0 %copy-done.2 = bf16[2048,128]{1,0:T(8,128)(2,1)S(1)} copy-done((bf16[2048,128]{1,0:T(8,128)(2,1)S(1)}, bf16[2048,128]{1,0:T(8,128)(2,1)}, u32[]{:S(2)}) %copy-start.2) | copy-done | bytes 524312
  5.1 28.9 %shard_map.77 = (f32[512,128]{1,0:T(8,128)S(1)}, f32[8,128]{1,0:T(8,128)S(1)}) custom-call(s32[8]{0:T(128)S(1)} %copy-done.4, s32[1]{0:T(128)S(6)} %copy.10.level_ref, s32[4,128]{1,0:T(4,128)S(1)} %bitcast.1, bf16[2048,128]{1,0:T(8,128)(2,1)S(1)} %copy-done, bf16[2048,128]{1,0:T(8,128)(2,1)S(1)} %copy-done.1, bf16[2048,128]{1,0:T(8,128)(2,1)S(1)} %copy-done.2), custom_call_target="tpu_custom_call" | custom-call | tf_op jit(solution)/shard_map/pallas_call | solution.py:265
  34.0 0.7 %copy.11 = f32[512,128]{1,0:T(8,128)} copy(f32[512,128]{1,0:T(8,128)S(1)} %get-tuple-element.4) | data formatting | bytes 524288
  34.7 0.6 %copy.12 = f32[8,128]{1,0:T(8,128)} copy(f32[8,128]{1,0:T(8,128)S(1)} %get-tuple-element.5) | data formatting | bytes 8192
Async XLA Ops:
  0.6 0.7 %copy-start.3 = (s32[512]{0:T(512)S(1)}, s32[512]{0:T(512)}, u32[]{:S(2)}) copy-start(s32[512]{0:T(512)} %param.10) | copy-start | bytes 6148
  1.3 0.7 %copy-start.4 = (s32[8]{0:T(128)S(1)}, s32[8]{0:T(128)}, u32[]{:S(2)}) copy-start(s32[8]{0:T(128)} %pos_ref.1) | copy-start | bytes 100
  2.0 1.0 %copy-start = (bf16[2048,128]{1,0:T(8,128)(2,1)S(1)}, bf16[2048,128]{1,0:T(8,128)(2,1)}, u32[]{:S(2)}) copy-start(bf16[2048,128]{1,0:T(8,128)(2,1)} %keys_hbm.1) | copy-start | bytes 1572868
  3.0 1.0 %copy-start.1 = (bf16[2048,128]{1,0:T(8,128)(2,1)S(1)}, bf16[2048,128]{1,0:T(8,128)(2,1)}, u32[]{:S(2)}) copy-start(bf16[2048,128]{1,0:T(8,128)(2,1)} %values_hbm.1) | copy-start | bytes 1572868
  4.0 1.0 %copy-start.2 = (bf16[2048,128]{1,0:T(8,128)(2,1)S(1)}, bf16[2048,128]{1,0:T(8,128)(2,1)}, u32[]{:S(2)}) copy-start(bf16[2048,128]{1,0:T(8,128)(2,1)} %queries_hbm.1) | copy-start | bytes 1572868

commit v2 on v1

--- a/solution.py
+++ b/solution.py
@@ -20,12 +20,16 @@
     )
 
 
-def inverse_block(m):
+def inverse_start(m):
+    return m, m[:SUB, :]
+
+
+def inverse_steps(state, first, last):
+    m, rows = state
     sub = lax.broadcasted_iota(jnp.int32, (SUB, LANES), 0)
     lane = lax.broadcasted_iota(jnp.int32, (SUB, LANES), 1)
     wide_lane = lax.broadcasted_iota(jnp.int32, (LANES, LANES), 1)
-    for s in range(0, LANES, SUB):
-        rows = m[s : s + SUB, :]
+    for s in range(first, last, SUB):
         cols = [jnp.broadcast_to(rows[:, s + j : s + j + 1], (SUB, LANES)) for j in range(SUB)]
         inside = (lane >= s) & (lane < s + SUB)
         work = jnp.where(inside, jnp.where(lane - s == sub, 1.0, 0.0), rows)
@@ -38,20 +42,35 @@
                 cols[j] = jnp.where(here, scaled, cols[j] - factor * scaled)
             scaled = work[i : i + 1, :] * pivot
             work = jnp.where(here, scaled, work - factor * scaled)
-        panel = m[:, s : s + SUB]
-        cleared = jnp.where((wide_lane >= s) & (wide_lane < s + SUB), 0.0, m)
+        after = s + SUB
+        if after < LANES:
+            coming = m[after : after + SUB, :]
+            terms = [
+                jnp.broadcast_to(coming[:, s + j : s + j + 1], (SUB, LANES)) * work[j : j + 1, :]
+                for j in range(SUB)
+            ]
+            while len(terms) > 1:
+                terms = [x + y for x, y in zip(terms[::2], terms[1::2])]
+            rows = jnp.where(inside, 0.0, coming) - terms[0]
+        panel = m[:, s:after]
+        cleared = jnp.where((wide_lane >= s) & (wide_lane < after), 0.0, m)
         m = cleared - jnp.dot(panel, work, precision=HIGH, preferred_element_type=jnp.float32)
-        parts = ([m[:s]] if s else []) + [work] + ([m[s + SUB :]] if s + SUB < LANES else [])
+        parts = [m[:s]] if s else []
+        parts.append(work)
+        if after < LANES:
+            parts.append(rows)
+        if after + SUB < LANES:
+            parts.append(m[after + SUB :])
         m = jnp.concatenate(parts, axis=0)
-    return m
+    return m, rows
+
+
+def inverse_block(m):
+    return inverse_steps(inverse_start(m), 0, LANES)[0]
 
 
 def invert(s_ref):
     count = s_ref.shape[0]
-    if count == LANES:
-        s_ref[...] = inverse_block(s_ref[...])
-        return
-
     def turn(k, carry):
         at = pl.ds(pl.multiple_of(k * LANES, LANES), LANES)
         inner = inverse_block(s_ref[at, at])
@@ -78,14 +97,17 @@
 
 def kernel(
     n,
-    pos_ref,
-    level_ref,
-    kept_ref,
+    pos_hbm,
+    level_hbm,
+    kept_hbm,
     keys_hbm,
     values_hbm,
     queries_hbm,
     matched_ref,
     ref_ref,
+    pos_ref,
+    level_ref,
+    kept_ref,
     keys,
     values,
     queries,
@@ -115,7 +137,16 @@
 
     loads = [
         pltpu.make_async_copy(src, dst, load_sem.at[k])
-        for k, (src, dst) in enumerate(((queries_hbm, queries), (keys_hbm, keys), (values_hbm, values)))
+        for k, (src, dst) in enumerate(
+            (
+                (pos_hbm, pos_ref),
+                (queries_hbm, queries),
+                (kept_hbm, kept_ref),
+                (keys_hbm, keys),
+                (values_hbm, values),
+                (level_hbm, level_ref),
+            )
+        )
     ]
     for load in loads:
         load.start()
@@ -169,6 +200,7 @@
     ref_args = (4, lambda p: own_ref, all_ref)
 
     loads[0].wait()
+    loads[1].wait()
     sub = lax.broadcasted_iota(jnp.int32, (own, slab), 0)
     wanted = jnp.zeros((own, slab), jnp.int32)
     for i in range(own):
@@ -180,7 +212,8 @@
     own_q[...] = rows
     all_q[me] = rows
 
-    loads[1].wait()
+    loads[2].wait()
+    loads[3].wait()
     places = lax.broadcasted_iota(jnp.int32, (LANES, slab), 1).astype(jnp.float32)
     for j in range(keep // LANES):
         offset = (kept_ref[j : j + 1, :] - start).astype(jnp.float32)
@@ -205,7 +238,7 @@
     kept_all[me] = total.astype(chunk.dtype)
     send(*kept_args)
 
-    loads[2].wait()
+    loads[4].wait()
     scores = nt(all_queries, keys[...]) * inv_root
     peak = jnp.max(scores, axis=1, keepdims=True)
     probs = jnp.exp(scores - peak).astype(jnp.bfloat16)
@@ -223,6 +256,16 @@
     weights = jnp.exp(logits - jnp.max(logits, axis=1, keepdims=True))
     weights = weights / jnp.sum(weights, axis=1, keepdims=True)
 
+    loads[5].wait()
+    ridge = level_ref[0].astype(jnp.float32) * 0.01
+    eye = lax.broadcasted_iota(jnp.int32, (count, count), 0) == lax.broadcasted_iota(
+        jnp.int32, (count, count), 1
+    )
+    system[...] = nt(weights, weights, HIGH) + jnp.where(eye, ridge, 0.0)
+    single = count == LANES
+    if single:
+        state = inverse_steps(inverse_start(system[...]), 0, LANES // 2)
+
     arrive(*part_args)
     stats = part_in[:, :, head_dim:]
     peaks = stats[:, :, 0:1]
@@ -234,12 +277,10 @@
     ref_ref[...] = merged
     send(*ref_args)
 
-    ridge = level_ref[0].astype(jnp.float32) * 0.01
-    eye = lax.broadcasted_iota(jnp.int32, (count, count), 0) == lax.broadcasted_iota(
-        jnp.int32, (count, count), 1
-    )
-    system[...] = nt(weights, weights, HIGH) + jnp.where(eye, ridge, 0.0)
-    invert(system)
+    if single:
+        system[...] = inverse_steps(state, LANES // 2, LANES)[0]
+    else:
+        invert(system)
 
     arrive(*ref_args)
     full_ref = all_ref[...].reshape(count, head_dim)
@@ -259,8 +300,7 @@
     each = keep // n
     link = jnp.bfloat16 if each % 16 == 0 else jnp.float32
     vmem = pl.BlockSpec(memory_space=pltpu.VMEM)
-    smem = pl.BlockSpec(memory_space=pltpu.SMEM)
-    hbm = pl.BlockSpec(memory_space=pl.ANY)
+    hbm = pl.BlockSpec(memory_space=pltpu.HBM)
     f32 = jnp.float32
     return pl.pallas_call(
         functools.partial(kernel, n),
@@ -268,9 +308,12 @@
             jax.ShapeDtypeStruct((keep, head_dim), f32),
             jax.ShapeDtypeStruct((own, head_dim), f32),
         ),
-        in_specs=[smem, smem, vmem, hbm, hbm, hbm],
+        in_specs=[hbm] * 6,
         out_specs=(vmem, vmem),
         scratch_shapes=[
+            pltpu.SMEM((own,), jnp.int32),
+            pltpu.SMEM((1,), jnp.int32),
+            pltpu.VMEM((keep // LANES, LANES), jnp.int32),
             pltpu.VMEM((slab, head_dim), keys.dtype),
             pltpu.VMEM((slab, head_dim), values.dtype),
             pltpu.VMEM((slab, head_dim), queries.dtype),
@@ -285,7 +328,7 @@
             pltpu.VMEM((own, head_dim), f32),
             pltpu.VMEM((n, own, head_dim), f32),
             pltpu.VMEM((count, count), f32),
-            pltpu.SemaphoreType.DMA((3,)),
+            pltpu.SemaphoreType.DMA((6,)),
             pltpu.SemaphoreType.DMA((5, n)),
             pltpu.SemaphoreType.DMA((5, n)),
         ],

time: 35.6 us -> 35.9 us (level)
  no operation moved by 1% of the time
where the time goes in v2:
time: 35.9 us; the launch traced here: 35.6 us
  Pallas kernels  29.2 us (81%)
  local copies, waits for them, and re-layouts  5.07 us (14%)
  between operations  1.32 us (4%)
    pallas_call x1, Pallas kernels, per_device(): pl.pallas_call(functools.partial(kernel, n), out_shape=(jax.ShapeDtypeStr...  29.2 us
    unnamed x12, local copies, waits for them, and re-layouts  5.07 us

profile of v2, /device:TPU:0, one launch (start us, length us, event | category | flops | bytes accessed | tf_op | source)
XLA Modules:
  0.0 35.6 jit_solution(2849633128641776412)
XLA Ops:
  0.6 0.0 copy-start.3
  1.3 0.0 copy-start.4
  1.3 0.0 copy-done.3
  1.3 0.6 %copy-done.4 = s32[8]{0:T(128)S(1)} copy-done((s32[8]{0:T(128)S(1)}, s32[8]{0:T(128)}, u32[]{:S(2)}) %copy-start.4) | copy-done | bytes 56
  2.0 0.0 copy-start
  2.0 1.0 %copy-done = bf16[2048,128]{1,0:T(8,128)(2,1)S(1)} copy-done((bf16[2048,128]{1,0:T(8,128)(2,1)S(1)}, bf16[2048,128]{1,0:T(8,128)(2,1)}, u32[]{:S(2)}) %copy-start) | copy-done | bytes 524312
  3.0 0.0 copy-start.1
  3.0 1.0 %copy-done.1 = bf16[2048,128]{1,0:T(8,128)(2,1)S(1)} copy-done((bf16[2048,128]{1,0:T(8,128)(2,1)S(1)}, bf16[2048,128]{1,0:T(8,128)(2,1)}, u32[]{:S(2)}) %copy-start.1) | copy-done | bytes 524312
  4.0 0.0 copy-start.2
  4.0 1.0 %copy-done.2 = bf16[2048,128]{1,0:T(8,128)(2,1)S(1)} copy-done((bf16[2048,128]{1,0:T(8,128)(2,1)S(1)}, bf16[2048,128]{1,0:T(8,128)(2,1)}, u32[]{:S(2)}) %copy-start.2) | copy-done | bytes 524312
  5.1 29.2 %shard_map.77 = (f32[512,128]{1,0:T(8,128)S(1)}, f32[8,128]{1,0:T(8,128)S(1)}) custom-call(s32[8]{0:T(128)S(1)} %copy-done.4, s32[1]{0:T(128)S(6)} %copy.10.level_hbm, s32[4,128]{1,0:T(4,128)S(1)} %bitcast.1, bf16[2048,128]{1,0:T(8,128)(2,1)S(1)} %copy-done, bf16[2048,128]{1,0:T(8,128)(2,1)S(1)} %copy-done.1, bf16[2048,128]{1,0:T(8,128)(2,1)S(1)} %copy-done.2), custom_call_target="tpu_custom_call" | custom-call | tf_op jit(solution)/shard_map/pallas_call | solution.py:305
  34.3 0.7 %copy.11 = f32[512,128]{1,0:T(8,128)} copy(f32[512,128]{1,0:T(8,128)S(1)} %get-tuple-element.4) | data formatting | bytes 524288
  35.0 0.6 %copy.12 = f32[8,128]{1,0:T(8,128)} copy(f32[8,128]{1,0:T(8,128)S(1)} %get-tuple-element.5) | data formatting | bytes 8192
Async XLA Ops:
  0.6 0.7 %copy-start.3 = (s32[512]{0:T(512)S(1)}, s32[512]{0:T(512)}, u32[]{:S(2)}) copy-start(s32[512]{0:T(512)} %param.10) | copy-start | bytes 6148
  1.3 0.7 %copy-start.4 = (s32[8]{0:T(128)S(1)}, s32[8]{0:T(128)}, u32[]{:S(2)}) copy-start(s32[8]{0:T(128)} %pos_hbm.1) | copy-start | bytes 100
  2.0 1.0 %copy-start = (bf16[2048,128]{1,0:T(8,128)(2,1)S(1)}, bf16[2048,128]{1,0:T(8,128)(2,1)}, u32[]{:S(2)}) copy-start(bf16[2048,128]{1,0:T(8,128)(2,1)} %keys_hbm.1) | copy-start | bytes 1572868
  3.0 1.0 %copy-start.1 = (bf16[2048,128]{1,0:T(8,128)(2,1)S(1)}, bf16[2048,128]{1,0:T(8,128)(2,1)}, u32[]{:S(2)}) copy-start(bf16[2048,128]{1,0:T(8,128)(2,1)} %values_hbm.1) | copy-start | bytes 1572868
  4.0 1.0 %copy-start.2 = (bf16[2048,128]{1,0:T(8,128)(2,1)S(1)}, bf16[2048,128]{1,0:T(8,128)(2,1)}, u32[]{:S(2)}) copy-start(bf16[2048,128]{1,0:T(8,128)(2,1)} %queries_hbm.1) | copy-start | bytes 1572868

commit v3 on v2

--- a/solution.py
+++ b/solution.py
@@ -244,9 +244,14 @@
     probs = jnp.exp(scores - peak).astype(jnp.bfloat16)
     totals = jnp.sum(probs.astype(jnp.float32), axis=1, keepdims=True)
     numer = jnp.dot(probs, values[...], preferred_element_type=jnp.float32)
-    half = lax.broadcasted_iota(jnp.int32, (count, LANES), 1) < LANES // 2
-    part[:, :, :head_dim] = numer.reshape(n, own, head_dim)
-    part[:, :, head_dim:] = jnp.where(half, peak, totals).reshape(n, own, LANES)
+    lane = lax.broadcasted_iota(jnp.int32, (n, own, LANES), 2)
+    place = lax.broadcasted_iota(jnp.int32, (n, own, LANES), 1)
+    stats = jnp.where(lane == place, jnp.broadcast_to(peak, (count, LANES)).reshape(n, own, LANES), 0.0)
+    stats = jnp.where(
+        lane == place + own, jnp.broadcast_to(totals, (count, LANES)).reshape(n, own, LANES), stats
+    )
+    part[:, :own, :] = numer.reshape(n, own, head_dim)
+    part[:, own:, :] = jnp.sum(stats, axis=1, keepdims=True)
     part_in[me] = part[me]
     send(*part_args)
 
@@ -267,11 +272,11 @@
         state = inverse_steps(inverse_start(system[...]), 0, LANES // 2)
 
     arrive(*part_args)
-    stats = part_in[:, :, head_dim:]
-    peaks = stats[:, :, 0:1]
-    sums = stats[:, :, LANES // 2 : LANES // 2 + 1]
+    stats = jnp.broadcast_to(part_in[:, own:, :], (n, own, LANES))
+    peaks = jnp.sum(jnp.where(lane == place, stats, 0.0), axis=2, keepdims=True)
+    sums = jnp.sum(jnp.where(lane == place + own, stats, 0.0), axis=2, keepdims=True)
     factors = jnp.exp(peaks - jnp.max(peaks, axis=0, keepdims=True))
-    merged = jnp.sum(part_in[:, :, :head_dim] * factors, axis=0) / jnp.sum(sums * factors, axis=0)
+    merged = jnp.sum(part_in[:, :own, :] * factors, axis=0) / jnp.sum(sums * factors, axis=0)
     own_ref[...] = merged
     all_ref[me] = merged
     ref_ref[...] = merged
@@ -300,7 +305,7 @@
     each = keep // n
     link = jnp.bfloat16 if each % 16 == 0 else jnp.float32
     vmem = pl.BlockSpec(memory_space=pltpu.VMEM)
-    hbm = pl.BlockSpec(memory_space=pltpu.HBM)
+    hbm = pl.BlockSpec(memory_space=pl.ANY)
     f32 = jnp.float32
     return pl.pallas_call(
         functools.partial(kernel, n),
@@ -323,8 +328,8 @@
             pltpu.VMEM((n, each, head_dim), link),
             pltpu.VMEM((each, head_dim), link),
             pltpu.VMEM((n, each, head_dim), link),
-            pltpu.VMEM((n, own, head_dim + LANES), f32),
-            pltpu.VMEM((n, own, head_dim + LANES), f32),
+            pltpu.VMEM((n, own + 1, head_dim), f32),
+            pltpu.VMEM((n, own + 1, head_dim), f32),
             pltpu.VMEM((own, head_dim), f32),
             pltpu.VMEM((n, own, head_dim), f32),
             pltpu.VMEM((count, count), f32),
@@ -333,7 +338,7 @@
             pltpu.SemaphoreType.DMA((5, n)),
         ],
         compiler_params=pltpu.CompilerParams(
-            collective_id=0, has_side_effects=True, vmem_limit_bytes=48 * 1024 * 1024
+            collective_id=0, has_side_effects=True, vmem_limit_bytes=61000 * 1024
         ),
     )(
         query_positions,

time: 35.9 us -> 32.8 us (0.914)
  local copies, waits for them, and re-layouts: 5.07 us -> 2.27 us
    unnamed x12 -> x4, local copies, waits for them, and re-layouts: 5.07 us -> 2.27 us
where the time goes in v3:
time: 32.8 us; the launch traced here: 32.6 us
  Pallas kernels  29 us (88%)
  local copies, waits for them, and re-layouts  2.27 us (7%)
  between operations  1.29 us (4%)
    pallas_call x1, Pallas kernels, per_device(): pl.pallas_call(functools.partial(kernel, n), out_shape=(jax.ShapeDtypeStr...  29 us
    unnamed x4, local copies, waits for them, and re-layouts  2.27 us

profile of v3, /device:TPU:0, one launch (start us, length us, event | category | flops | bytes accessed | tf_op | source)
XLA Modules:
  0.0 32.6 jit_solution(8508038512140145130)
XLA Ops:
  1.3 29.0 %shard_map.77 = (f32[512,128]{1,0:T(8,128)}, f32[8,128]{1,0:T(8,128)}) custom-call(s32[8]{0:T(128)} %pos_hbm.1, s32[1]{0:T(128)S(6)} %copy.10.level_hbm, s32[4,128]{1,0:T(4,128)} %bitcast.1, bf16[2048,128]{1,0:T(8,128)(2,1)} %keys_hbm.1, bf16[2048,128]{1,0:T(8,128)(2,1)} %values_hbm.1, bf16[2048,128]{1,0:T(8,128)(2,1)} %queries_hbm.1), custom_call_target="tpu_custom_call" | custom-call | tf_op jit(solution)/shard_map/pallas_call | solution.py:310
  30.3 0.0 copy-start
  30.3 1.7 %copy.11 = f32[512,128]{1,0:T(8,128)} copy(f32[512,128]{1,0:T(8,128)} %get-tuple-element.4) | data formatting | bytes 524288
  32.0 0.0 copy-done
  32.0 0.6 %copy.12 = f32[8,128]{1,0:T(8,128)} copy(f32[8,128]{1,0:T(8,128)S(1)} %copy-done) | data formatting | bytes 8192
Async XLA Ops:
  30.3 1.7 %copy-start = (f32[8,128]{1,0:T(8,128)S(1)}, f32[8,128]{1,0:T(8,128)}, u32[]{:S(2)}) copy-start(f32[8,128]{1,0:T(8,128)} %get-tuple-element.5) | copy-start | bytes 12292

commit v4 on v3

--- a/solution.py
+++ b/solution.py
@@ -173,11 +173,12 @@
         )
 
     def send(stage, src, dst):
-        def one(k, c):
+        def one(j, c):
+            k = n // 2 + (j + 1) // 2 * (1 - j % 2 * 2)
             copy_of(stage, k, src, dst).start()
             return c
 
-        lax.fori_loop(1, n, one, 0)
+        lax.fori_loop(0, n - 1, one, 0)
 
     def arrive(stage, src, dst):
         def one(k, c):
@@ -226,10 +227,8 @@
     pick_in[me] = pick[me]
 
     pl.semaphore_wait(barrier, n - 1)
+    send(*pick_args)
     send(*q_args)
-    send(*pick_args)
-    arrive(*q_args)
-    all_queries = all_q[...].reshape(count, head_dim).astype(jnp.bfloat16)
     arrive(*pick_args)
     total = pick_in[0].astype(jnp.float32)
     for k in range(1, n):
@@ -238,6 +237,8 @@
     kept_all[me] = total.astype(chunk.dtype)
     send(*kept_args)
 
+    arrive(*q_args)
+    all_queries = all_q[...].reshape(count, head_dim).astype(jnp.bfloat16)
     loads[4].wait()
     scores = nt(all_queries, keys[...]) * inv_root
     peak = jnp.max(scores, axis=1, keepdims=True)

time: 32.8 us -> 32 us (0.976)
  Pallas kernels: 29 us -> 28.3 us
    pallas_call x1, Pallas kernels: 29 us -> 28.3 us  [per_device(): pl.pallas_call(functools.partial(kernel, n), out_shape=(jax.ShapeDtypeStr...]
where the time goes in v4:
time: 32 us; the launch traced here: 31.8 us
  Pallas kernels  28.3 us (88%)
  local copies, waits for them, and re-layouts  2.27 us (7%)
  between operations  1.29 us (4%)
    pallas_call x1, Pallas kernels, per_device(): pl.pallas_call(functools.partial(kernel, n), out_shape=(jax.ShapeDtypeStr...  28.3 us
    unnamed x4, local copies, waits for them, and re-layouts  2.27 us

profile of v4, /device:TPU:0, one launch (start us, length us, event | category | flops | bytes accessed | tf_op | source)
XLA Modules:
  0.0 31.8 jit_solution(9488768365787245219)
XLA Ops:
  1.3 28.3 %shard_map.77 = (f32[512,128]{1,0:T(8,128)}, f32[8,128]{1,0:T(8,128)}) custom-call(s32[8]{0:T(128)} %pos_hbm.1, s32[1]{0:T(128)S(6)} %copy.10.level_hbm, s32[4,128]{1,0:T(4,128)} %bitcast.1, bf16[2048,128]{1,0:T(8,128)(2,1)} %keys_hbm.1, bf16[2048,128]{1,0:T(8,128)(2,1)} %values_hbm.1, bf16[2048,128]{1,0:T(8,128)(2,1)} %queries_hbm.1), custom_call_target="tpu_custom_call" | custom-call | tf_op jit(solution)/shard_map/pallas_call | solution.py:311
  29.6 0.0 copy-start
  29.6 1.7 %copy.11 = f32[512,128]{1,0:T(8,128)} copy(f32[512,128]{1,0:T(8,128)} %get-tuple-element.4) | data formatting | bytes 524288
  31.2 0.0 copy-done
  31.2 0.6 %copy.12 = f32[8,128]{1,0:T(8,128)} copy(f32[8,128]{1,0:T(8,128)S(1)} %copy-done) | data formatting | bytes 8192
Async XLA Ops:
  29.6 1.7 %copy-start = (f32[8,128]{1,0:T(8,128)S(1)}, f32[8,128]{1,0:T(8,128)}, u32[]{:S(2)}) copy-start(f32[8,128]{1,0:T(8,128)} %get-tuple-element.5) | copy-start | bytes 12292
